TPU v7x, 32 devices: a whole 2x2x4 slice. The times are simulated.
32 devices in a mesh: row: 8 (over y, x, core), col: 4 (over z).
Axes of the slice: x: 2, y: 2, z: 4, core: 2. Of those that a mesh axis runs over, the one named last changes fastest.
Arguments:
- design: bfloat16 [512, 90112], P(('row', 'col')), may hold values from -6 to 6
- arc_partials: float32 [32, 6, 16], P(('row', 'col')), may hold values from -6 to 6
- arc_id: int32 [32], P(('row', 'col')), may hold values from 0 to 7
- arc_weight: float32 [8], replicated, may hold values from 0.25 to 4
Outputs:
- normal_slab: float32 [90112, 2048], P('row', 'col')
All inputs are finite; a program needn't handle non-finite values.
Results may differ from a plain program's by a relative error of at most 0.0003.
The roundings to bfloat16 on the way count: a program that leaves them out, or rounds other values in their place, can miss the bound.
Values may be sent and summed in bfloat16 or wider, within the bound.
A program may use at most 128 MiB of HBM per device.

v0:
```python
import jax
import jax.numpy as jnp
from jax import lax
from jax.sharding import PartitionSpec as P

SLAB = 2048
ridge = 4.0


def solve_small(matrix, rhs):
    order = matrix.shape[-1]
    for pivot in range(order):
        scale = 1.0 / matrix[..., pivot, pivot]
        row_mat = matrix[..., pivot, :] * scale[..., None]
        row_rhs = rhs[..., pivot, :] * scale[..., None]
        factor = matrix[..., :, pivot]
        matrix = matrix - factor[..., :, None] * row_mat[..., None, :]
        rhs = rhs - factor[..., :, None] * row_rhs[..., None, :]
        matrix = matrix.at[..., pivot, :].set(row_mat)
        rhs = rhs.at[..., pivot, :].set(row_rhs)
    return rhs


def own_reduced(design, arc_partials, arc_id, arc_weight):
    high = lax.Precision.HIGHEST
    slab_rows = design[:, :SLAB].astype(jnp.float32)
    partials = arc_partials[0]
    coupling = jnp.dot(partials, slab_rows, precision=high, preferred_element_type=jnp.float32)
    gram = jnp.dot(partials, partials.T, precision=high, preferred_element_type=jnp.float32)
    arc_count = arc_weight.shape[0]
    select = (jnp.arange(arc_count) == arc_id[0]).astype(jnp.float32)
    arc_gram, arc_coupling = lax.psum(
        (select[:, None, None] * gram[None], select[:, None, None] * coupling[None]), ("row", "col")
    )
    order = partials.shape[0]
    own_gram = jnp.sum(select[:, None, None] * arc_gram, axis=0) + ridge * jnp.eye(
        order, dtype=jnp.float32
    )
    own_coupling = jnp.sum(select[:, None, None] * arc_coupling, axis=0)
    solved = solve_small(own_gram, own_coupling)
    reduced = slab_rows - jnp.dot(
        partials.T, solved, precision=high, preferred_element_type=jnp.float32
    )
    weight = jnp.sum(select * arc_weight)
    return (weight * reduced).astype(jnp.bfloat16)


def make_accumulate(ordered, piece):
    return lax.dot_general(
        piece, ordered, (((0,), (0,)), ((), ())), preferred_element_type=jnp.float32
    )


def col_major(slab_global, row_count, col_count, rows_dev):
    width = slab_global.shape[1]
    ordered = slab_global.reshape(row_count, col_count, rows_dev, width)
    return ordered.transpose(1, 0, 2, 3).reshape(rows_dev * row_count * col_count, width)


def local(design, arc_partials, arc_id, arc_weight):
    rows_dev = design.shape[0]
    row_count = lax.axis_size("row")
    col_count = lax.axis_size("col")
    devices = row_count * col_count
    epochs = rows_dev * devices
    eliminated_own = own_reduced(design, arc_partials, arc_id, arc_weight)
    regrouped = lax.all_to_all(design, "row", split_axis=1, concat_axis=0, tiled=True)
    columns = lax.all_to_all(eliminated_own, "col", split_axis=1, concat_axis=0, tiled=True)
    slab_global = lax.all_gather(columns, "row", axis=0, tiled=True)
    ordered = col_major(slab_global, row_count, col_count, rows_dev)
    normal = make_accumulate(ordered, lax.all_gather(regrouped, "col", axis=0, tiled=True))
    return normal * (1.0 / epochs)


def solution(mesh):
    placed = (P(("row", "col"), None), P(("row", "col"), None, None), P(("row", "col")), P())
    return jax.shard_map(
        local, mesh=mesh, in_specs=placed, out_specs=P("row", "col"), check_vma=False
    )
```

profile of v0, /device:TPU:0, one launch (start us, length us, event | category | flops | bytes accessed | tf_op | source)
XLA Modules:
  0.0 400.1 jit_solution(14108734418693655313)
XLA Ops:
  7.4 3.6 copy.42
  11.0 5.2 %all-to-all-start.1 = ((bf16[16,8,11264]{2,0,1:T(8,128)(2,1)}), bf16[16,8,11264]{2,0,1:T(8,128)(2,1)S(1)}, u32[]{:S(2)}, u32[]{:S(2)}) async-start(bf16[16,8,11264]{2,0,1:T(8,128)(2,1)} %bitcast.64), calls=%async_computation.1 | async-start | bytes 5767168 | tf_op jit(solution)/shard_map/all_to_all | solution.py:67
  16.9 1.0 fusion.3
  17.9 0.8 broadcast_multiply_fusion
  18.8 33.2 %all-to-all-done.1 = bf16[16,8,11264]{2,0,1:T(8,128)(2,1)S(1)} async-done(((bf16[16,8,11264]{2,0,1:T(8,128)(2,1)}), bf16[16,8,11264]{2,0,1:T(8,128)(2,1)S(1)}, u32[]{:S(2)}, u32[]{:S(2)}) %all-to-all-start.1) | async-done | bytes 2883616 | tf_op jit(solution)/shard_map/all_to_all | solution.py:67
  52.0 1.6 copy-done
  53.8 50.2 %psum.15 = f32[8,6,6]{2,0,1:T(8,128)S(1)} all-reduce(f32[8,6,6]{2,0,1:T(8,128)S(1)} %broadcast_multiply_fusion.1), channel_id=1, replica_groups=mesh['row'=8,'col'=4] {'row','col'}, use_global_device_ids=true, to_apply=%region_3.0 | all-reduce | flops 288 | bytes 2304 | tf_op jit(solution)/shard_map/psum | solution.py:32
  104.1 0.5 slice.240
  105.5 0.6 slice.244
  107.1 0.6 slice.248
  108.7 0.6 slice.252
  110.3 0.6 slice.256
  111.8 0.6 slice.260
  113.2 0.6 fusion.12
  114.0 216.3 %all-reduce.2.cloned.1.call-done = f32[8,6,2048]{2,0,1:T(8,128)} async-done(((f32[8,6,2048]{2,0,1:T(8,128)}), f32[8,6,2048]{2,0,1:T(8,128)}) %all-reduce.2.cloned.1.call-update) | async-done | bytes 393232 | tf_op jit(solution)/shard_map/psum | solution.py:32
  330.3 1.2 multiply_reduce_fusion
  331.6 0.2 scatter.36
  331.9 0.2 scatter.40
  332.1 0.2 scatter.44
  333.2 1.7 fusion.2
  334.9 9.2 %all_to_all.38 = bf16[16,4,512]{2,0,1:T(8,128)(2,1)S(1)} all-to-all(bf16[16,4,512]{2,0,1:T(8,128)(2,1)S(1)} %bitcast.70), channel_id=1, replica_groups=mesh['row'=8,'col'=4] {'col'}, dimensions={1} | all-to-all | bytes 131072 | tf_op jit(solution)/shard_map/all_to_all | solution.py:68
  344.1 9.8 %all_gather.6 = bf16[512,512]{1,0:T(8,128)(2,1)S(1)} all-gather(bf16[64,512]{1,0:T(8,128)(2,1)S(1)} %bitcast.69), channel_id=1, replica_groups=mesh['row'=8,'col'=4] {'row'}, dimensions={0}, use_global_device_ids=true | all-gather | bytes 589824 | tf_op jit(solution)/shard_map/all_gather | solution.py:69
  354.0 15.2 %multiply_bitcast_fusion = f32[11264,512]{0,1:T(8,128)} fusion(bf16[512,512]{1,0:T(8,128)(2,1)S(1)} %bitcast.65, bf16[512,11264]{1,0:T(8,128)(2,1)} %all-gather.2.cloned.1.call-done), kind=kOutput, calls=%fused_computation | convolution fusion | flops 5911347200 | bytes 35127296 | tf_op jit(solution)/shard_map/dot_general | solution.py:49
  369.1 23.5 %copy.24 = f32[11264,512]{1,0:T(8,128)} copy(f32[11264,512]{0,1:T(8,128)} %multiply_bitcast_fusion) | data formatting | bytes 46137344 | tf_op jit(solution)/shard_map/mul | solution.py:72
  (58 shorter events, 3.2 us)
Async XLA Ops:
  7.4 9.5 %copy-start.1 = (f32[1,6,16]{2,0,1:T(1,128)S(1)}, f32[1,6,16]{2,0,1:T(1,128)}, u32[]{:S(2)}) copy-start(f32[1,6,16]{2,0,1:T(1,128)} %param.27) | copy-start | bytes 1156
  7.4 105.8 %copy-start.2 = (f32[8]{0:T(128)S(1)}, f32[8]{0:T(128)}, u32[]{:S(2)}) copy-start(f32[8]{0:T(128)} %param.29) | copy-start | bytes 100
  11.0 41.0 %all-to-all-start.1 = ((bf16[16,8,11264]{2,0,1:T(8,128)(2,1)}), bf16[16,8,11264]{2,0,1:T(8,128)(2,1)S(1)}, u32[]{:S(2)}, u32[]{:S(2)}) async-start(bf16[16,8,11264]{2,0,1:T(8,128)(2,1)} %bitcast.64), calls=%async_computation.1 | async-start | bytes 5767168 | tf_op jit(solution)/shard_map/all_to_all | solution.py:67
  16.2 314.1 %all-reduce.2.cloned.1.call-start = ((), (), s32[]{:S(2)}) async-start(), calls=%async_computation.2 | async-start | bytes 786432 | tf_op jit(solution)/shard_map/psum | solution.py:32
  18.8 335.2 %all-gather.2.cloned.1.call-start = ((), (), s32[]{:S(2)}) async-start(), calls=%async_computation.3 | async-start | bytes 14417920 | tf_op jit(solution)/shard_map/all_gather | solution.py:71
  52.0 1.6 copy-start
Sparse Core Ops, SparseCore 0:
  22.3 307.9 all-reduce.1
Sparse Core Ops, SparseCore 1:
  53.7 201.6 all-gather.1
where the time goes:
time: 401 us; the launch traced here: 400 us
  waiting for transfers between devices  250 us (62%)
  blocking collectives  69.1 us (17%)
  local copies, waits for them, and re-layouts  34.6 us (9%)
  between operations  19.7 us (5%)
  matrix products  18 us (4%)
  starting transfers between devices  5.28 us (1%)
    psum x1, waiting for transfers between devices, own_reduced(): lax.psum((select[:, None, None] * gram[None], select[:, None, None] * cou...  216 us
    psum x1, blocking collectives, own_reduced(): lax.psum((select[:, None, None] * gram[None], select[:, None, None] * cou...  50.2 us
    all_to_all x1, waiting for transfers between devices, local(): lax.all_to_all(design, 'row', split_axis=1, concat_axis=0, tiled=True)  33.2 us
    mul x1, local copies, waits for them, and re-layouts, local(): return normal * (1.0 / epochs)  23.5 us
    dot_general x1, matrix products, make_accumulate(): lax.dot_general(piece, ordered, (((0,), (0,)), ((), ())), preferred_eleme...  15.2 us
    all_gather x1, blocking collectives, local(): slab_global = lax.all_gather(columns, 'row', axis=0, tiled=True)  9.79 us
    all_to_all x1, blocking collectives, local(): lax.all_to_all(eliminated_own, 'col', split_axis=1, concat_axis=0, tiled=...  9.18 us
  transfers between devices with their start and end apart: 3, of which 2 were waited for; matrix products, arithmetic and copies ran while one was open for 3% of the time, Pallas kernels for 0%

commit v1 on v0

--- a/solution.py
+++ b/solution.py
@@ -64,7 +64,10 @@
     devices = row_count * col_count
     epochs = rows_dev * devices
     eliminated_own = own_reduced(design, arc_partials, arc_id, arc_weight)
-    regrouped = lax.all_to_all(design, "row", split_axis=1, concat_axis=0, tiled=True)
+    regrouped = jnp.concatenate(
+        lax.all_to_all(jnp.stack(jnp.split(design, lax.axis_size("row"), axis=1)), "row", 0, 0),
+        axis=0,
+    )
     columns = lax.all_to_all(eliminated_own, "col", split_axis=1, concat_axis=0, tiled=True)
     slab_global = lax.all_gather(columns, "row", axis=0, tiled=True)
     ordered = col_major(slab_global, row_count, col_count, rows_dev)

time: 401 us -> 389 us (0.970)
  local copies, waits for them, and re-layouts: 34.6 us -> 21.3 us
    mul x1 -> x0, local copies, waits for them, and re-layouts: 23.5 us -> none  [local(): return normal * (1.0 / epochs)]
    unnamed x6 -> x13, local copies, waits for them, and re-layouts: 1.58 us -> 13.8 us
where the time goes in v1:
time: 389 us; the launch traced here: 388 us
  waiting for transfers between devices  250 us (64%)
  blocking collectives  69.1 us (18%)
  local copies, waits for them, and re-layouts  21.3 us (5%)
  between operations  19.5 us (5%)
  matrix products  18.7 us (5%)
  starting transfers between devices  5.42 us (1%)
    psum x1, waiting for transfers between devices, own_reduced(): lax.psum((select[:, None, None] * gram[None], select[:, None, None] * cou...  217 us
    psum x1, blocking collectives, own_reduced(): lax.psum((select[:, None, None] * gram[None], select[:, None, None] * cou...  50.1 us
    all_to_all x1, waiting for transfers between devices, local(): lax.all_to_all(jnp.stack(jnp.split(design, lax.axis_size('row'), axis=1))...  33.2 us
    dot_general x1, matrix products, make_accumulate(): lax.dot_general(piece, ordered, (((0,), (0,)), ((), ())), preferred_eleme...  15.7 us
    unnamed x13, local copies, waits for them, and re-layouts  13.8 us
    all_gather x1, blocking collectives, local(): slab_global = lax.all_gather(columns, 'row', axis=0, tiled=True)  9.79 us
    all_to_all x1, blocking collectives, local(): lax.all_to_all(eliminated_own, 'col', split_axis=1, concat_axis=0, tiled=...  9.17 us
  transfers between devices with their start and end apart: 3, of which 2 were waited for; matrix products, arithmetic and copies ran while one was open for 3% of the time, Pallas kernels for 0%

profile of v1, /device:TPU:0, one launch (start us, length us, event | category | flops | bytes accessed | tf_op | source)
XLA Modules:
  0.0 387.7 jit_solution(4442606546653077290)
XLA Ops:
  7.4 1.7 bitcast_dynamic-update-slice_fusion.7
  9.1 1.7 bitcast_dynamic-update-slice_fusion.6
  10.9 1.7 bitcast_dynamic-update-slice_fusion.5
  12.6 1.7 bitcast_dynamic-update-slice_fusion.4
  14.3 1.7 bitcast_dynamic-update-slice_fusion.3
  16.1 1.7 bitcast_dynamic-update-slice_fusion.2
  17.8 1.7 bitcast_dynamic-update-slice_fusion.1
  19.6 1.7 bitcast_dynamic-update-slice_fusion
  21.3 5.3 %all-to-all-start = ((bf16[8,16,11264]{2,1,0:T(8,128)(2,1)}), bf16[8,16,11264]{2,1,0:T(8,128)(2,1)S(1)}, u32[]{:S(2)}, u32[]{:S(2)}) async-start(bf16[8,16,11264]{2,1,0:T(8,128)(2,1)} %bitcast_dynamic-update-slice_fusion), calls=%async_computation | async-start | bytes 5767168 | tf_op jit(solution)/shard_map/all_to_all | solution.py:68
  27.4 1.0 fusion.3
  28.4 0.9 broadcast_multiply_fusion
  29.3 33.2 %all-to-all-done = bf16[8,16,11264]{2,1,0:T(8,128)(2,1)S(1)} async-done(((bf16[8,16,11264]{2,1,0:T(8,128)(2,1)}), bf16[8,16,11264]{2,1,0:T(8,128)(2,1)S(1)}, u32[]{:S(2)}, u32[]{:S(2)}) %all-to-all-start) | async-done | bytes 2883616 | tf_op jit(solution)/shard_map/all_to_all | solution.py:68
  62.5 1.6 copy-done
  64.3 50.1 %psum.15 = f32[8,6,6]{2,0,1:T(8,128)S(1)} all-reduce(f32[8,6,6]{2,0,1:T(8,128)S(1)} %broadcast_multiply_fusion.1), channel_id=1, replica_groups=mesh['row'=8,'col'=4] {'row','col'}, use_global_device_ids=true, to_apply=%region_3.0 | all-reduce | flops 288 | bytes 2304 | tf_op jit(solution)/shard_map/psum | solution.py:32
  115.9 0.6 slice.244
  117.4 0.6 slice.248
  120.5 0.6 slice.256
  123.3 0.7 fusion.12
  124.1 216.6 %all-reduce.2.cloned.1.call-done = f32[8,6,2048]{2,0,1:T(8,128)} async-done(((f32[8,6,2048]{2,0,1:T(8,128)}), f32[8,6,2048]{2,0,1:T(8,128)}) %all-reduce.2.cloned.1.call-update) | async-done | bytes 393232 | tf_op jit(solution)/shard_map/psum | solution.py:32
  340.7 1.2 multiply_reduce_fusion
  343.6 1.8 fusion.2
  345.5 9.2 %all_to_all.24 = bf16[16,4,512]{2,0,1:T(8,128)(2,1)S(1)} all-to-all(bf16[16,4,512]{2,0,1:T(8,128)(2,1)S(1)} %bitcast.76), channel_id=1, replica_groups=mesh['row'=8,'col'=4] {'col'}, dimensions={1} | all-to-all | bytes 131072 | tf_op jit(solution)/shard_map/all_to_all | solution.py:71
  354.7 9.8 %all_gather.7 = bf16[512,512]{1,0:T(8,128)(2,1)S(1)} all-gather(bf16[64,512]{1,0:T(8,128)(2,1)S(1)} %bitcast.75), channel_id=1, replica_groups=mesh['row'=8,'col'=4] {'row'}, dimensions={0}, use_global_device_ids=true | all-gather | bytes 589824 | tf_op jit(solution)/shard_map/all_gather | solution.py:72
  364.5 15.7 %convolution_multiply_fusion = f32[11264,512]{1,0:T(8,128)} fusion(bf16[512,11264]{1,0:T(8,128)(2,1)} %all-gather.2.cloned.1.call-done, bf16[512,512]{1,0:T(8,128)(2,1)S(1)} %bitcast.73), kind=kOutput, calls=%fused_computation | convolution fusion | flops 5911347200 | bytes 35127296 | tf_op jit(solution)/shard_map/dot_general | solution.py:49
  (64 shorter events, 5.4 us)
Async XLA Ops:
  21.3 6.0 %copy-start.1 = (f32[1,6,16]{2,0,1:T(1,128)S(1)}, f32[1,6,16]{2,0,1:T(1,128)}, u32[]{:S(2)}) copy-start(f32[1,6,16]{2,0,1:T(1,128)} %param.27) | copy-start | bytes 1156
  21.3 41.2 %all-to-all-start = ((bf16[8,16,11264]{2,1,0:T(8,128)(2,1)}), bf16[8,16,11264]{2,1,0:T(8,128)(2,1)S(1)}, u32[]{:S(2)}, u32[]{:S(2)}) async-start(bf16[8,16,11264]{2,1,0:T(8,128)(2,1)} %bitcast_dynamic-update-slice_fusion), calls=%async_computation | async-start | bytes 5767168 | tf_op jit(solution)/shard_map/all_to_all | solution.py:68
  26.6 96.6 %copy-start.2 = (f32[8]{0:T(128)S(1)}, f32[8]{0:T(128)}, u32[]{:S(2)}) copy-start(f32[8]{0:T(128)} %param.29) | copy-start | bytes 100
  26.6 314.1 %all-reduce.2.cloned.1.call-start = ((), (), s32[]{:S(2)}) async-start(), calls=%async_computation.3 | async-start | bytes 786432 | tf_op jit(solution)/shard_map/psum | solution.py:32
  29.2 335.3 %all-gather.2.cloned.1.call-start = ((), (), s32[]{:S(2)}) async-start(), calls=%async_computation.2 | async-start | bytes 14417920 | tf_op jit(solution)/shard_map/all_gather | solution.py:74
  62.5 1.6 copy-start
Sparse Core Ops, SparseCore 0:
  32.8 307.9 all-reduce.1
Sparse Core Ops, SparseCore 1:
  64.2 201.6 all-gather.1
